TPU v7x, 32 devices: a whole 2x2x4 slice. The times are simulated.
32 devices in a mesh: va: 8 (over y, x, core), vb: 4 (over z).
Axes of the slice: x: 2, y: 2, z: 4, core: 2. Of those that a mesh axis runs over, the one named last changes fastest.
Arguments:
- clique_a: float32 [16, 8, 2, 16, 32768], P('va', 'vb'), may hold values from 0.2 to 5
- message_in: float32 [16, 2, 32768], P('va'), may hold values from 0.2 to 5
- clique_b: float32 [32, 8, 16, 16, 8, 256], P(None, None, None, 'va', 'vb'), may hold values from 0.2 to 5
- old_separator: float32 [8, 16, 16, 8, 256], P(None, None, 'va', 'vb'), may hold values from 0.25 to 4
Outputs:
- absorbed: float32 [16, 8, 2, 16, 32768], P('va', 'vb')
- updated_b: float32 [32, 8, 16, 16, 8, 256], P(None, None, None, 'va', 'vb')
- onward: float32 [32, 16, 16, 256], P('vb', None, 'va')
All inputs are finite; a program needn't handle non-finite values.
Results may differ from a plain program's by a relative error of at most 0.00002.
Values sent between devices are 32-bit elements; how exact they have to be, the bound alone decides.
No kernel may reach another device: no remote copies, remote signals or barrier semaphores. Data moves between devices by JAX's collectives and lax.ppermute only.
A program may use at most 192 MiB of HBM per device.

v0:
```python
import jax
import jax.numpy as jnp
from jax import lax
from jax.sharding import PartitionSpec as P

H = 16
K = 2
P_SIZE = 8
R1 = 16
R2 = 8
R3 = 256


def body(clique_a, message_in, clique_b, old_separator):
    p_local = clique_a.shape[1]
    q_total = clique_a.shape[3]
    r_total = clique_a.shape[4]
    absorbed = clique_a * message_in[:, None, :, None, :]
    column_width = r_total // R1
    summed = jnp.sum(absorbed, axis=(0, 2)) * (1.0 / (H * K))
    summed = summed.reshape(
        p_local, q_total, lax.axis_size("va") * (R1 // lax.axis_size("va")), column_width
    )
    shares = lax.psum_scatter(
        jnp.transpose(summed, (2, 0, 1, 3)), "va", scatter_dimension=0, tiled=True
    )
    shares = shares.reshape(shares.shape[0], p_local, q_total, R2, R3)
    moved = lax.all_to_all(shares, "vb", split_axis=3, concat_axis=1, tiled=True)
    separator = jnp.transpose(moved, (1, 2, 0, 3, 4))
    scaling = separator / old_separator
    updated_b = clique_b * scaling[None]
    partial_value = jnp.sum(updated_b, axis=(1, 4)) * (1.0 / (P_SIZE * R2))
    onward = lax.psum_scatter(partial_value, "vb", scatter_dimension=0, tiled=True)
    return (absorbed, updated_b, onward)


def solution(mesh):
    return jax.shard_map(
        body,
        mesh=mesh,
        in_specs=(
            P("va", "vb", None, None, None),
            P("va", None, None),
            P(None, None, None, "va", "vb", None),
            P(None, None, "va", "vb", None),
        ),
        out_specs=(
            P("va", "vb", None, None, None),
            P(None, None, None, "va", "vb", None),
            P("vb", None, "va", None),
        ),
        check_vma=False,
    )
```

profile of v0, /device:TPU:0, one launch (start us, length us, event | category | flops | bytes accessed | tf_op | source)
XLA Modules:
  0.0 156.1 jit_solution(7697594367874494386)
XLA Ops:
  7.2 0.0 reduce-scatter.3.cloned.1.call-start
  7.2 12.5 %fusion.1 = (f32[2,16,32768]{2,1,0:T(8,128)S(1)}, f32[2,2,2,16,32768]{4,3,2,1,0:T(8,128)}) fusion(f32[2,2,2,16,32768]{4,3,2,1,0:T(8,128)} %param.4, f32[2,2,32768]{2,1,0:T(2,128)} %param.5), kind=kLoop, calls=%fused_computation.8 | loop fusion | flops 7340032 | bytes 38273024 | tf_op jit(solution)/shard_map/reduce_sum | solution.py:20
  19.7 0.3 broadcast_multiply_fusion.2
  19.9 0.0 copy-start
  19.9 2.4 %copy.41 = f32[4,8,16,2048]{3,2,1,0:T(8,128)S(1)} copy(f32[4,8,16,2048]{3,1,2,0:T(8,128)S(1)} %bitcast.18) | data formatting | bytes 8388608
  22.4 0.5 bitcast_bitcast_fusion
  22.9 4.4 %copy.31 = f32[16,2,16,2048]{3,2,1,0:T(8,128)} copy(f32[16,2,16,2048]{3,0,2,1:T(8,128)S(1)} %bitcast_bitcast_fusion) | data formatting | bytes 8388608 | tf_op jit(solution)/shard_map/transpose | solution.py:25
  27.3 0.0 reduce-scatter.3.cloned.1.call-update
  27.4 0.0 reduce-scatter.5.cloned.1.call-start
  27.4 54.1 %reduce-scatter.3.cloned.1.call-done = f32[2,2,16,2048]{3,2,1,0:T(8,128)} async-done(((f32[16,2,16,2048]{3,2,1,0:T(8,128)}), f32[2,2,16,2048]{3,2,1,0:T(8,128)}) %reduce-scatter.3.cloned.1.call-update) | async-done | bytes 524304 | tf_op jit(solution)/shard_map/reduce_scatter | solution.py:24
  81.5 1.1 copy.45
  82.6 18.9 %all_to_all.18 = f32[2,2,16,8,256]{4,2,1,0,3:T(8,128)S(1)} all-to-all(f32[2,2,16,8,256]{4,2,1,0,3:T(8,128)S(1)} %bitcast.21), channel_id=1, replica_groups=mesh['va'=8,'vb'=4] {'vb'}, dimensions={3} | all-to-all | bytes 1048576 | tf_op jit(solution)/shard_map/all_to_all | solution.py:28
  101.6 0.0 copy-done
  101.6 0.1 copy_divide_fusion
  101.7 0.4 copy.36
  102.1 18.7 %fusion = (f32[32,16,2,256]{3,2,1,0:T(2,128)S(1)}, f32[32,8,16,2,2,256]{5,4,3,2,1,0:T(2,128)}) fusion(f32[32,8,16,2,2,256]{5,4,3,2,1,0:T(2,128)} %param.6, f32[8,16,2,2,256]{4,3,2,1,0:T(2,128)S(1)} %copy.36), kind=kLoop, calls=%fused_computation.7 | loop fusion | flops 8126464 | bytes 35127296 | tf_op jit(solution)/shard_map/reduce_sum | solution.py:32
  120.9 1.1 copy_multiply_fusion
  122.0 0.0 reduce-scatter.5.cloned.1.call-update
  122.0 25.4 %reduce-scatter.5.cloned.1.call-done = f32[8,16,2,256]{3,1,2,0:T(8,128)} async-done(((f32[32,16,2,256]{3,1,2,0:T(8,128)}), f32[8,16,2,256]{3,1,2,0:T(8,128)}) %reduce-scatter.5.cloned.1.call-update) | async-done | bytes 262160 | tf_op jit(solution)/shard_map/reduce_scatter | solution.py:33
  147.5 1.9 %copy.38 = f32[8,16,2,256]{3,2,1,0:T(2,128)} copy(f32[8,16,2,256]{3,1,2,0:T(8,128)} %reduce-scatter.5.cloned.1.call-done) | data formatting | bytes 524288
  (1 shorter events, 0.0 us)
Async XLA Ops:
  7.2 74.4 %reduce-scatter.3.cloned.1.call-start = ((), (), s32[]{:S(2)}) async-start(), calls=%async_computation.3 | async-start | bytes 4718592 | tf_op jit(solution)/shard_map/reduce_scatter | solution.py:24
  19.9 81.6 %copy-start = (f32[8,16,2,2,256]{4,3,2,1,0:T(2,128)S(1)}, f32[8,16,2,2,256]{4,3,2,1,0:T(2,128)}, u32[]{:S(2)}) copy-start(f32[8,16,2,2,256]{4,3,2,1,0:T(2,128)} %param.7) | copy-start | bytes 1572868
  27.4 120.1 %reduce-scatter.5.cloned.1.call-start = ((), (), s32[]{:S(2)}) async-start(), calls=%async_computation.4 | async-start | bytes 1310720 | tf_op jit(solution)/shard_map/reduce_scatter | solution.py:33
Sparse Core Ops, SparseCore 0:
  27.5 53.9 reduce-scatter.2
  122.2 25.2 reduce-scatter.4
where the time goes:
time: 156 us
  waiting for transfers between devices  79.6 us (51%)
  other arithmetic  32.7 us (21%)
  blocking collectives  18.9 us (12%)
  between operations  14.1 us (9%)
  local copies, waits for them, and re-layouts  10.8 us (7%)
    reduce_scatter x1, waiting for transfers between devices, body(): lax.psum_scatter(jnp.transpose(summed, (2, 0, 1, 3)), 'va', scatter_dimen...  54.1 us
    reduce_scatter x1, waiting for transfers between devices, body(): lax.psum_scatter(partial_value, 'vb', scatter_dimension=0, tiled=True)  25.4 us
    all_to_all x1, blocking collectives, body(): lax.all_to_all(shares, 'vb', split_axis=3, concat_axis=1, tiled=True)  18.9 us
    reduce_sum x1, other arithmetic, body(): partial_value = jnp.sum(updated_b, axis=(1, 4)) * (1.0 / (P_SIZE * R2))  18.7 us
    reduce_sum x1, other arithmetic, body(): summed = jnp.sum(absorbed, axis=(0, 2)) * (1.0 / (H * K))  12.5 us
    transpose x2, local copies, waits for them, and re-layouts, body(): jnp.transpose(summed, (2, 0, 1, 3))  4.93 us
    unnamed x4, local copies, waits for them, and re-layouts  4.29 us
  transfers between devices with their start and end apart: 2, of which 2 were waited for; matrix products, arithmetic and copies ran while one was open for 0% of the time, Pallas kernels for 0%

commit v1 on v0

--- a/solution.py
+++ b/solution.py
@@ -25,7 +25,19 @@
         jnp.transpose(summed, (2, 0, 1, 3)), "va", scatter_dimension=0, tiled=True
     )
     shares = shares.reshape(shares.shape[0], p_local, q_total, R2, R3)
-    moved = lax.all_to_all(shares, "vb", split_axis=3, concat_axis=1, tiled=True)
+    ways, here = (lax.axis_size("vb"), lax.axis_index("vb"))
+    width = shares.shape[3] // ways
+    shape = list(shares.shape)
+    shape[3] = width
+    height = shape[1]
+    shape[1] = height * ways
+    full = jnp.zeros(shape, shares.dtype)
+    for mask in range(ways):
+        part = lax.dynamic_slice_in_dim(shares, (here ^ mask) * width, width, axis=3)
+        if mask:
+            part = lax.ppermute(part, "vb", [(d, d ^ mask) for d in range(ways)])
+        full = lax.dynamic_update_slice_in_dim(full, part, (here ^ mask) * height, axis=1)
+    moved = full
     separator = jnp.transpose(moved, (1, 2, 0, 3, 4))
     scaling = separator / old_separator
     updated_b = clique_b * scaling[None]

time: 156 us -> 154 us (0.987)
  blocking collectives: 18.9 us -> 0 us
  waiting for transfers between devices: 79.6 us -> 90.7 us
  starting transfers between devices: 0.08 us -> 4.53 us
    all_to_all x1 -> x0, blocking collectives: 18.9 us -> none  [body(): lax.all_to_all(shares, 'vb', split_axis=3, concat_axis=1, tiled=True)]
    ppermute x0 -> x3, waiting for transfers between devices: none -> 9.82 us  [body(): part = lax.ppermute(part, 'vb', [(d, d ^ mask) for d in range(ways)])]
    ppermute x0 -> x3, starting transfers between devices: none -> 4.45 us  [body(): part = lax.ppermute(part, 'vb', [(d, d ^ mask) for d in range(ways)])]
    unnamed x4 -> x8, local copies, waits for them, and re-layouts: 4.29 us -> 5.57 us
  transfers between devices with their start and end apart: 2 -> 5, of which waited for: 2 -> 4; matrix products, arithmetic and copies ran while one was open for 0% -> 0% of each run, Pallas kernels for 0% -> 0%
where the time goes in v1:
time: 154 us; the launch traced here: 153 us
  waiting for transfers between devices  90.7 us (59%)
  other arithmetic  32.9 us (21%)
  between operations  14.2 us (9%)
  local copies, waits for them, and re-layouts  11 us (7%)
  starting transfers between devices  4.53 us (3%)
    reduce_scatter x1, waiting for transfers between devices, body(): lax.psum_scatter(jnp.transpose(summed, (2, 0, 1, 3)), 'va', scatter_dimen...  54.1 us
    reduce_scatter x1, waiting for transfers between devices, body(): lax.psum_scatter(partial_value, 'vb', scatter_dimension=0, tiled=True)  26.8 us
    reduce_sum x1, other arithmetic, body(): partial_value = jnp.sum(updated_b, axis=(1, 4)) * (1.0 / (P_SIZE * R2))  18.7 us
    reduce_sum x1, other arithmetic, body(): summed = jnp.sum(absorbed, axis=(0, 2)) * (1.0 / (H * K))  12.5 us
    ppermute x3, waiting for transfers between devices, body(): part = lax.ppermute(part, 'vb', [(d, d ^ mask) for d in range(ways)])  9.82 us
    unnamed x8, local copies, waits for them, and re-layouts  5.57 us
    transpose x2, local copies, waits for them, and re-layouts, body(): jnp.transpose(summed, (2, 0, 1, 3))  4.93 us
    ppermute x3, starting transfers between devices, body(): part = lax.ppermute(part, 'vb', [(d, d ^ mask) for d in range(ways)])  4.45 us
  transfers between devices with their start and end apart: 5, of which 4 were waited for; matrix products, arithmetic and copies ran while one was open for 0% of the time, Pallas kernels for 0%

profile of v1, /device:TPU:0, one launch (start us, length us, event | category | flops | bytes accessed | tf_op | source)
XLA Modules:
  0.0 153.3 jit_solution(8405900124823397670)
XLA Ops:
  7.2 0.0 reduce-scatter.3.cloned.1.call-start
  7.2 12.5 %fusion.1 = (f32[2,16,32768]{2,1,0:T(8,128)S(1)}, f32[2,2,2,16,32768]{4,3,2,1,0:T(8,128)}) fusion(f32[2,2,2,16,32768]{4,3,2,1,0:T(8,128)} %param.4, f32[2,2,32768]{2,1,0:T(2,128)} %param.5), kind=kLoop, calls=%fused_computation.15 | loop fusion | flops 7340032 | bytes 38273024 | tf_op jit(solution)/shard_map/reduce_sum | solution.py:20
  19.7 0.3 broadcast_multiply_fusion.2
  19.9 0.0 copy-start
  19.9 2.4 %copy.36 = f32[4,8,16,2048]{3,2,1,0:T(8,128)S(1)} copy(f32[4,8,16,2048]{3,1,2,0:T(8,128)S(1)} %bitcast.15) | data formatting | bytes 8388608
  22.4 0.5 bitcast_bitcast_fusion
  22.9 4.4 %copy.25 = f32[16,2,16,2048]{3,2,1,0:T(8,128)} copy(f32[16,2,16,2048]{3,0,2,1:T(8,128)S(1)} %bitcast_bitcast_fusion) | data formatting | bytes 8388608 | tf_op jit(solution)/shard_map/transpose | solution.py:25
  27.3 0.0 reduce-scatter.3.cloned.1.call-update
  27.4 0.0 reduce-scatter.5.cloned.1.call-start
  27.4 54.1 %reduce-scatter.3.cloned.1.call-done = f32[2,2,16,2048]{3,2,1,0:T(8,128)} async-done(((f32[16,2,16,2048]{3,2,1,0:T(8,128)}), f32[2,2,16,2048]{3,2,1,0:T(8,128)}) %reduce-scatter.3.cloned.1.call-update) | async-done | bytes 524304 | tf_op jit(solution)/shard_map/reduce_scatter | solution.py:24
  81.5 1.2 copy.37
  82.7 0.2 constant_dynamic-slice_fusion
  83.1 1.5 %collective-permute-start = (f32[2,2,16,2,256]{4,3,0,2,1:T(2,128)S(1)}, f32[2,2,16,2,256]{4,3,0,2,1:T(2,128)S(1)}, u32[]{:S(2)}, u32[]{:S(2)}) collective-permute-start(f32[2,2,16,2,256]{4,3,0,2,1:T(2,128)S(1)} %copy.33), channel_id=1, source_target_pairs={{0,1},{1,0},{2,3},{3,2},{4,5},{5,4},{6,7},{7,6},{8,9},{9,8},{10,11... | collective-permute-start | bytes 393224 | tf_op jit(solution)/shard_map/ppermute | solution.py:38
  84.6 2.4 %collective-permute-start.1 = (f32[2,2,16,2,256]{4,3,0,2,1:T(2,128)S(1)}, f32[2,2,16,2,256]{4,3,0,2,1:T(2,128)S(1)}, u32[]{:S(2)}, u32[]{:S(2)}) collective-permute-start(f32[2,2,16,2,256]{4,3,0,2,1:T(2,128)S(1)} %copy.34), channel_id=1, source_target_pairs={{0,2},{1,3},{2,0},{3,1},{4,6},{5,7},{6,4},{7,5},{8,10},{9,11},{10,... | collective-permute-start | bytes 393224 | tf_op jit(solution)/shard_map/ppermute | solution.py:38
  87.0 0.5 collective-permute-start.2
  87.5 0.1 broadcast_in_dim.2
  87.7 2.3 %collective-permute-done = f32[2,2,16,2,256]{4,3,0,2,1:T(2,128)S(1)} collective-permute-done((f32[2,2,16,2,256]{4,3,0,2,1:T(2,128)S(1)}, f32[2,2,16,2,256]{4,3,0,2,1:T(2,128)S(1)}, u32[]{:S(2)}, u32[]{:S(2)}) %collective-permute-start) | collective-permute-done | bytes 131104 | tf_op jit(solution)/shard_map/ppermute | solution.py:38
  90.0 7.6 %collective-permute-done.1 = f32[2,2,16,2,256]{4,3,0,2,1:T(2,128)S(1)} collective-permute-done((f32[2,2,16,2,256]{4,3,0,2,1:T(2,128)S(1)}, f32[2,2,16,2,256]{4,3,0,2,1:T(2,128)S(1)}, u32[]{:S(2)}, u32[]{:S(2)}) %collective-permute-start.1) | collective-permute-done | bytes 131104 | tf_op jit(solution)/shard_map/ppermute | solution.py:38
  97.6 0.0 collective-permute-done.2
  97.6 0.0 copy-done
  97.6 0.3 bitcast_divide_fusion
  97.9 18.7 %fusion = (f32[32,16,2,256]{3,2,1,0:T(2,128)S(1)}, f32[32,8,16,2,2,256]{5,4,3,2,1,0:T(2,128)}) fusion(f32[32,8,16,2,2,256]{5,4,3,2,1,0:T(2,128)} %param.6, f32[8,16,2,2,256]{4,3,2,1,0:T(2,128)S(1)} %bitcast_divide_fusion), kind=kLoop, calls=%fused_computation.14 | loop fusion | flops 8126464 | bytes 35127296 | tf_op jit(solution)/shard_map/reduce_sum | solution.py:44
  116.7 1.1 copy_multiply_fusion
  117.8 0.0 reduce-scatter.5.cloned.1.call-update
  117.8 26.8 %reduce-scatter.5.cloned.1.call-done = f32[8,16,2,256]{3,1,2,0:T(8,128)} async-done(((f32[32,16,2,256]{3,1,2,0:T(8,128)}), f32[8,16,2,256]{3,1,2,0:T(8,128)}) %reduce-scatter.5.cloned.1.call-update) | async-done | bytes 262160 | tf_op jit(solution)/shard_map/reduce_scatter | solution.py:45
  144.6 1.9 %copy.31 = f32[8,16,2,256]{3,2,1,0:T(2,128)} copy(f32[8,16,2,256]{3,1,2,0:T(8,128)} %reduce-scatter.5.cloned.1.call-done) | data formatting | bytes 524288
  (7 shorter events, 0.2 us)
Async XLA Ops:
  7.2 74.4 %reduce-scatter.3.cloned.1.call-start = ((), (), s32[]{:S(2)}) async-start(), calls=%async_computation.2 | async-start | bytes 4718592 | tf_op jit(solution)/shard_map/reduce_scatter | solution.py:24
  19.9 77.7 %copy-start = (f32[8,16,2,2,256]{4,3,2,1,0:T(2,128)S(1)}, f32[8,16,2,2,256]{4,3,2,1,0:T(2,128)}, u32[]{:S(2)}) copy-start(f32[8,16,2,2,256]{4,3,2,1,0:T(2,128)} %param.7) | copy-start | bytes 1572868
  27.4 117.3 %reduce-scatter.5.cloned.1.call-start = ((), (), s32[]{:S(2)}) async-start(), calls=%async_computation.3 | async-start | bytes 1310720 | tf_op jit(solution)/shard_map/reduce_scatter | solution.py:45
  83.1 6.9 %collective-permute-start = (f32[2,2,16,2,256]{4,3,0,2,1:T(2,128)S(1)}, f32[2,2,16,2,256]{4,3,0,2,1:T(2,128)S(1)}, u32[]{:S(2)}, u32[]{:S(2)}) collective-permute-start(f32[2,2,16,2,256]{4,3,0,2,1:T(2,128)S(1)} %copy.33), channel_id=1, source_target_pairs={{0,1},{1,0},{2,3},{3,2},{4,5},{5,4},{6,7},{7,6},{8,9},{9,8},{10,11... | collective-permute-start | bytes 393224 | tf_op jit(solution)/shard_map/ppermute | solution.py:38
  84.6 12.9 %collective-permute-start.1 = (f32[2,2,16,2,256]{4,3,0,2,1:T(2,128)S(1)}, f32[2,2,16,2,256]{4,3,0,2,1:T(2,128)S(1)}, u32[]{:S(2)}, u32[]{:S(2)}) collective-permute-start(f32[2,2,16,2,256]{4,3,0,2,1:T(2,128)S(1)} %copy.34), channel_id=1, source_target_pairs={{0,2},{1,3},{2,0},{3,1},{4,6},{5,7},{6,4},{7,5},{8,10},{9,11},{10,... | collective-permute-start | bytes 393224 | tf_op jit(solution)/shard_map/ppermute | solution.py:38
  87.0 10.5 %collective-permute-start.2 = (f32[2,2,16,2,256]{4,3,0,2,1:T(2,128)S(1)}, f32[2,2,16,2,256]{4,3,0,2,1:T(2,128)S(1)}, u32[]{:S(2)}, u32[]{:S(2)}) collective-permute-start(f32[2,2,16,2,256]{4,3,0,2,1:T(2,128)S(1)} %copy.35), channel_id=1, source_target_pairs={{0,3},{1,2},{2,1},{3,0},{4,7},{5,6},{6,5},{7,4},{8,11},{9,10},{10,... | collective-permute-start | bytes 393224 | tf_op jit(solution)/shard_map/ppermute | solution.py:38
Sparse Core Ops, SparseCore 0:
  27.5 53.9 reduce-scatter.2
  117.9 26.6 reduce-scatter.4
